TPU v7x, 32 devices: a whole 2x2x4 slice. The times are simulated.
32 devices in a mesh: seq: 8 (over z, x), head: 4 (over y, core).
Axes of the slice: x: 2, y: 2, z: 4, core: 2. Of those that a mesh axis runs over, the one named last changes fastest.
Arguments:
- queries: float32 [2048, 8192], P('seq', 'head'), may hold values from -8 to 8
- key_heads: float32 [2048, 1024], P('seq', 'head'), may hold values from -6 to 6
- value_heads: float32 [2048, 1024], P('seq', 'head'), may hold values from -6 to 6
- query_map: float32 [64, 128, 128], P('head'), may hold values from -0.5 to 0.5
- key_map: float32 [8, 128, 128], P('head'), may hold values from -0.5 to 0.5
Outputs:
- query_map_step: float32 [64, 128, 128], P('head')
- key_map_step: float32 [8, 128, 128], P('head')
All inputs are finite; a program needn't handle non-finite values.
Results may differ from a plain program's by a relative error of at most 0.00019.
Values sent between devices are 32-bit elements; how exact they have to be, the bound alone decides.
No kernel may reach another device: no remote copies, remote signals or barrier semaphores. Data moves between devices by JAX's collectives and lax.ppermute only.
A program may use at most 64 MiB of HBM per device.

v0:
```python
import functools
import math

import jax
import jax.numpy as jnp
from jax import lax
from jax.experimental import pallas as pl
from jax.experimental.pallas import tpu as pltpu
from jax.sharding import PartitionSpec as P


EPSILON = 1e-06
F32 = jnp.float32
BF16 = jnp.bfloat16
LIMIT = 20 * 2**20
NN = (((1,), (0,)), ((), ()))
TN = (((0,), (0,)), ((), ()))


def split(x):
    hi = x.astype(BF16)
    lo = (x - hi.astype(F32)).astype(BF16)
    return hi, lo


def mm(a, b, dims=NN):
    return lax.dot_general(a, b, dims, preferred_element_type=F32)


def wide(x):
    return jnp.concatenate(split(x), axis=1)


def tall(hi):
    return jnp.concatenate([hi, hi], axis=0)


def fold(x):
    half = x.shape[1] // 2
    return x[:, :half] + x[:, half:]


def square(x):
    return tall(wide(x))


def softplus(x):
    return jnp.maximum(x, 0.0) + jnp.log1p(jnp.exp(-jnp.abs(x)))


def sigmoid(x):
    e = jnp.exp(-jnp.abs(x))
    r = 1.0 / (1.0 + e)
    return jnp.where(x >= 0.0, r, e * r)


def row_sum(x):
    return jnp.sum(x, axis=1, keepdims=True)


def attend_kernel(first, count, groups, pair, scale, flags, *refs):
    q_ref = refs[0]
    blocks = refs[1 : 1 + count]
    if first:
        qt_ref, stat_out, acc_out = refs[1 + count : 4 + count]
        keys, vals = refs[4 + count :]
    else:
        wk_ref, _, _, _, _ = refs[1 + count : 6 + count]
        stat_out, acc_out, st_out, nm_out, sig_out = refs[6 + count : 11 + count]
        keys, vals = refs[11 + count :]
    rows = blocks[0].shape[0]
    dh = blocks[0].shape[1] // (2 * groups)
    heads = acc_out.shape[0]
    steps = heads // groups // pair
    on = flags[0]
    for b in range(1, count):
        on = on + flags[b]

    def prepare(b):
        for g in range(groups):
            value = blocks[b][:, (groups + g) * dh : (groups + g + 1) * dh]
            key_wide = wide(blocks[b][:, g * dh : (g + 1) * dh])
            keys[g, b * rows : (b + 1) * rows, :] = key_wide
            vals[g, :, b * rows : (b + 1) * rows] = jnp.concatenate(split(value.T), axis=0)
            if not first:
                act = fold(mm(key_wide, square(wk_ref[g])))
                sig_out[b, g] = sigmoid(act)
                feat = softplus(act)
                fh, fl = split(feat)
                val_wide = wide(value)
                st_out[g] += fold(mm(fh, val_wide, TN)) + mm(fl, val_wide[:, :dh], TN)
                nm_out[g] += jnp.sum(feat.reshape(-1, 8, feat.shape[1]), axis=0)

    def update(begin, number):
        def some_heads(j, _):
            g = lax.div(j, steps)

            def scores(p):
                h = j * pair + p
                if first:
                    q = q_ref[:, pl.ds(pl.multiple_of(h * dh, dh), dh)] * scale
                    q_t = jnp.concatenate(split(q.T), axis=0)
                    qt_ref[h] = q_t
                else:
                    q_t = q_ref[h]
                q_hi, q_lo = tall(q_t[:dh]), q_t[dh:]
                found = []
                for b in range(number):
                    key = keys[g, (begin + b) * rows : (begin + b + 1) * rows, :]
                    s = mm(key, q_hi) + mm(key[:, :dh], q_lo)
                    if first:
                        before = lax.broadcasted_iota(jnp.int32, s.shape, 0) <= lax.broadcasted_iota(jnp.int32, s.shape, 1)
                        s = jnp.where(before, s, -1e30)
                    found.append(s)
                return found

            ahead = scores(0)
            for p in range(pair):
                h = j * pair + p
                now = ahead
                new = functools.reduce(jnp.maximum, [jnp.max(s, axis=0, keepdims=True) for s in now])
                if not first:
                    old = stat_out[h, 0:1, :]
                    new = jnp.maximum(old, new)
                    fade = jnp.exp2(old - new)
                if p + 1 < pair:
                    ahead = scores(p + 1)
                tot, out = 0.0, 0.0
                for b in range(number):
                    w = jnp.exp2(now[b] - new)
                    tot = tot + jnp.sum(w, axis=0, keepdims=True)
                    wh, wl = split(w)
                    val = vals[g, :, (begin + b) * rows : (begin + b + 1) * rows]
                    both = mm(val, wh)
                    out = out + both[:dh] + both[dh:] + mm(val[:dh], wl)
                if not first:
                    tot = tot + fade * stat_out[h, 1:2, :]
                    out = out + fade * acc_out[h]
                stat_out[h, 0:1, :] = new
                stat_out[h, 1:2, :] = tot
                acc_out[h] = out
            return 0

        lax.fori_loop(0, heads // pair, some_heads, 0)

    if first:
        prepare(0)
        update(0, 1)
        return

    @pl.when(on == count)
    def _():
        for b in range(count):
            prepare(b)
        update(0, count)

    if count > 1:
        for b in range(count):

            @pl.when(jnp.logical_and(on < count, flags[b] > 0))
            def _():
                prepare(b)
                update(b, 1)


def attend(q, blocks, flags, key_map, state, heads, pair):
    groups, dh, feat = key_map.shape
    rows = blocks[0].shape[0]
    count = len(blocks)
    first = state is None
    tokens = rows if first else q.shape[2]
    stat_shape = jax.ShapeDtypeStruct((heads, 2, tokens), F32)
    acc_shape = jax.ShapeDtypeStruct((heads, dh, tokens), F32)
    vmem = pl.BlockSpec(memory_space=pltpu.VMEM)
    smem = pl.BlockSpec(memory_space=pltpu.SMEM)
    alias = {}
    if first:
        args = [q, *blocks]
        out_shape = [jax.ShapeDtypeStruct((heads, 2 * dh, rows), BF16), stat_shape, acc_shape]
    else:
        args = [q, *blocks, key_map, *state]
        out_shape = [
            stat_shape,
            acc_shape,
            jax.ShapeDtypeStruct((groups, feat, dh), F32),
            jax.ShapeDtypeStruct((groups, 8, feat), F32),
            jax.ShapeDtypeStruct((count, groups, rows, feat), F32),
        ]
        alias = {3 + count + i: i for i in range(4)}
    scale = math.log2(math.e) * dh ** (-0.5)
    return pl.pallas_call(
        functools.partial(attend_kernel, first, count, groups, pair, scale),
        out_shape=out_shape,
        in_specs=[smem] + [vmem] * len(args),
        out_specs=[vmem] * len(out_shape),
        scratch_shapes=[
            pltpu.VMEM((groups, count * rows, 2 * dh), BF16),
            pltpu.VMEM((groups, 2 * dh, count * rows), BF16),
        ],
        input_output_aliases=alias,
        compiler_params=pltpu.CompilerParams(vmem_limit_bytes=LIMIT),
        cost_estimate=pl.CostEstimate(
            flops=heads * count * 24 * rows * tokens * dh,
            bytes_accessed=4 * tokens * dh * heads * 3,
            transcendentals=heads * count * rows * tokens,
        ),
        name="attend",
    )(flags, *args)


def causal_mask(rows):
    return lax.broadcasted_iota(jnp.int32, (rows, rows), 0) >= lax.broadcasted_iota(jnp.int32, (rows, rows), 1)


def local_kernel(groups, pair, *refs):
    q_ref, kv_ref, wq_ref, wk_ref, qf_ref, sig_ref, num_ref, part_ref, feat_ref, sig_k_ref, turned, turned_lo, val_w = refs
    heads, dh, feat_dim = wq_ref.shape
    rows = q_ref.shape[0]
    steps = heads // groups // pair
    for g in range(groups):
        act = fold(mm(wide(kv_ref[:, g * dh : (g + 1) * dh]), square(wk_ref[g])))
        feat = softplus(act)
        sig_k_ref[g] = sigmoid(act)
        hi, lo = split(feat.T)
        turned[g] = tall(hi)
        turned_lo[g] = lo
        feat_ref[g] = wide(feat)
        val_w[g] = wide(kv_ref[:, (groups + g) * dh : (groups + g + 1) * dh])
    causal = causal_mask(rows)

    def some_heads(j, _):
        g = lax.div(j, steps)
        each = [j * pair + p for p in range(pair)]
        q = [wide(q_ref[:, pl.ds(pl.multiple_of(h * dh, dh), dh)]) for h in each]
        act = [fold(mm(x, square(wq_ref[h]))) for x, h in zip(q, each)]
        qf = [wide(softplus(x)) for x in act]
        for x, y, h in zip(act, qf, each):
            sig_ref[h] = sigmoid(x)
            qf_ref[h] = y
        kern = [mm(x, turned[g]) + mm(x[:, :feat_dim], turned_lo[g]) for x in qf]
        kern = [jnp.where(causal, x, 0.0) for x in kern]
        for x, h in zip(kern, each):
            part_ref[h] = functools.reduce(
                jnp.add, [x[:, c : c + feat_dim] for c in range(0, rows, feat_dim)]
            )
        halves = [split(x) for x in kern]
        val = val_w[g]
        for (hi, lo), h in zip(halves, each):
            num_ref[h] = fold(mm(hi, val)) + mm(lo, val[:, :dh])
        return 0

    lax.fori_loop(0, heads // pair, some_heads, 0)


def vmem_call(kernel, args, out_shape, scratch, flops, first_smem=True):
    vmem = pl.BlockSpec(memory_space=pltpu.VMEM)
    smem = pl.BlockSpec(memory_space=pltpu.SMEM)
    return pl.pallas_call(
        kernel,
        out_shape=out_shape,
        in_specs=([smem] if first_smem else [vmem]) + [vmem] * (len(args) - 1),
        out_specs=[vmem] * len(out_shape),
        scratch_shapes=scratch,
        compiler_params=pltpu.CompilerParams(vmem_limit_bytes=LIMIT),
        cost_estimate=pl.CostEstimate(flops=flops, bytes_accessed=2**22, transcendentals=2**20),
    )(*args)


def local(q, own, query_map, key_map, pair):
    heads, dh, feat = query_map.shape
    groups = key_map.shape[0]
    rows = q.shape[0]
    shape = jax.ShapeDtypeStruct
    return vmem_call(
        functools.partial(local_kernel, groups, pair),
        [q, own, query_map, key_map],
        [
            shape((heads, rows, 2 * feat), BF16),
            shape((heads, rows, feat), F32),
            shape((heads, rows, dh), F32),
            shape((heads, rows, feat), F32),
            shape((groups, rows, 2 * feat), BF16),
            shape((groups, rows, feat), F32),
        ],
        [
            pltpu.VMEM((groups, 2 * feat, rows), BF16),
            pltpu.VMEM((groups, feat, rows), BF16),
            pltpu.VMEM((groups, rows, 2 * dh), BF16),
        ],
        heads * 24 * rows * rows * dh,
        first_smem=False,
    )


def learn_kernel(group, groups, counts, pair, outer, inner, flags, *refs):
    count = sum(counts)
    q_ref, kv_ref, st_ref, nm_ref, stat_ref, acc_ref = refs[:6]
    qf_ref, sig_ref, num_ref, part_ref, feat_ref, sig_k_ref = refs[6:12]
    blocks = refs[12 : 12 + count]
    sigs = refs[12 + count : 12 + count + len(counts)]
    outs = refs[12 + count + len(counts) : 12 + count + len(counts) + inner]
    val_t2, val_t_lo, st_sq, st_t_sq, adj, adj_n, result = refs[12 + count + len(counts) + inner :]
    heads, rows, dh = num_ref.shape
    feat_dim = sig_ref.shape[2]
    ratio = heads // groups
    total = outer * inner
    q_rows, k_rows = ratio * dh // total, dh // total
    outer_me, inner_me = flags[count], flags[count + 1]
    columns = slice(group * dh, (group + 1) * dh)
    val_columns = slice((groups + group) * dh, (groups + group + 1) * dh)

    def place(s):
        i, j = lax.div(s, inner), lax.rem(s, inner)
        return lax.rem(j - inner_me + inner, inner), lax.rem(i - outer_me + outer, outer)

    hi, lo = split(kv_ref[:, val_columns].T)
    val_t2[...] = tall(hi)
    val_t_lo[...] = lo
    st_sq[...] = square(st_ref[group])
    st_t_sq[...] = square(st_ref[group].T)
    adj[...] = jnp.zeros_like(adj)
    adj_n[...] = jnp.zeros_like(adj_n)
    norm_prev = jnp.sum(nm_ref[group], axis=0, keepdims=True)
    causal = causal_mask(rows)

    def some_heads(j, _):
        each = [group * ratio + j * pair + p for p in range(pair)]
        teacher = [(acc_ref[h] / stat_ref[h, 1:2, :]).T for h in each]
        qfw = [qf_ref[h] for h in each]
        qf = [x[:, :feat_dim].astype(F32) + x[:, feat_dim:].astype(F32) for x in qfw]
        num = [num_ref[h] + fold(mm(x, st_sq[...])) for x, h in zip(qfw, each)]
        inv = [1.0 / row_sum(part_ref[h] + x * norm_prev) for x, h in zip(qf, each)]
        student = [x * y for x, y in zip(num, inv)]
        mismatch = [x - y for x, y in zip(student, teacher)]
        gn = [wide(x * y) for x, y in zip(mismatch, inv)]
        gd = [-row_sum(x * y) * z for x, y, z in zip(mismatch, student, inv)]
        coupling = [mm(x, val_t2[...]) + mm(x[:, :dh], val_t_lo[...]) for x in gn]
        coupling = [split(jnp.where(causal, x + y, 0.0)) for x, y in zip(coupling, gd)]
        feat = feat_ref[group]
        gqf = [
            fold(mm(hi, feat)) + mm(lo, feat[:, :feat_dim]) + fold(mm(x, st_t_sq[...])) + y * norm_prev
            for (hi, lo), x, y in zip(coupling, gn, gd)
        ]
        for (hi, lo), x, y in zip(coupling, gn, qfw):
            left_hi = jnp.concatenate([hi, x[:, :dh]], axis=1)
            left_lo = jnp.concatenate([lo, x[:, dh:]], axis=1)
            adj[...] += fold(mm(left_hi, y, TN)) + mm(left_lo, y[:, :feat_dim], TN)
        for x, y in zip(qf, gd):
            adj_n[...] += jnp.sum((x * y).reshape(-1, 8, feat_dim), axis=0)
        back = [wide(x * sig_ref[h]) for x, h in zip(gqf, each)]
        for p, (x, h) in enumerate(zip(back, each)):
            hi, lo = split(q_ref[:, pl.ds(pl.multiple_of(h * dh, dh), dh)])
            grad = fold(mm(hi, x, TN)) + mm(lo, x[:, :feat_dim], TN)
            first = (j * pair + p) * (dh // q_rows)
            for k in range(dh // q_rows):
                e, f = place(first + k)
                result[e, f, :q_rows, :] = grad[k * q_rows : (k + 1) * q_rows]
        return 0

    lax.fori_loop(0, ratio // pair, some_heads, 0)

    def key_side(keys, x):
        xw = wide(x)
        hi, lo = split(keys)
        return fold(mm(hi, xw, TN)) + mm(lo, xw[:, :feat_dim], TN)

    adj_sq = square(adj[rows:])
    adj_norm = jnp.sum(adj_n[...], axis=0, keepdims=True)
    grad_k = key_side(kv_ref[:, columns], adj[:rows] * sig_k_ref[group])
    b = 0
    for stage, number in enumerate(counts):
        for k in range(number):
            grad = fold(mm(wide(blocks[b][:, val_columns]), adj_sq)) + adj_norm
            more = key_side(blocks[b][:, columns], grad * sigs[stage][k, group])
            grad_k = grad_k + jnp.where(flags[b] > 0, more, 0.0)
            b += 1
    for s in range(total):
        e, f = place(s)
        result[e, f, q_rows:, :] = grad_k[s * k_rows : (s + 1) * k_rows]
    for e in range(inner):
        outs[e][...] = result[e]


def learn(group, flags, q, own, state, mine, blocks, sigs, sizes, pair):
    groups, heads, outer, inner, dh, feat = sizes
    rows = own.shape[0]
    total = outer * inner
    share = (heads // groups + 1) * dh // total
    counts = tuple(x.shape[0] for x in sigs)
    stat, acc, st, nm = state
    args = [flags, q, own, st, nm, stat, acc, *mine, *blocks, *sigs]
    return vmem_call(
        functools.partial(learn_kernel, group, groups, counts, pair, outer, inner),
        args,
        [jax.ShapeDtypeStruct((outer, share, feat), F32)] * inner,
        [
            pltpu.VMEM((2 * dh, rows), BF16),
            pltpu.VMEM((dh, rows), BF16),
            pltpu.VMEM((2 * feat, 2 * dh), BF16),
            pltpu.VMEM((2 * dh, 2 * feat), BF16),
            pltpu.VMEM((rows + dh, feat), F32),
            pltpu.VMEM((8, feat), F32),
            pltpu.VMEM((inner, outer, share, feat), F32),
        ],
        heads // groups * 40 * rows * rows * dh,
    )


def pack_kernel(k_ref, v_ref, out_ref):
    width = k_ref.shape[1]
    out_ref[:, :width] = k_ref[...]
    out_ref[:, width:] = v_ref[...]


def piece_kernel(*refs):
    out = refs[-1]
    rows = refs[0].shape[0]
    value = functools.reduce(jnp.add, [r[...] for r in refs[:-1]])
    out[:rows, :] = value
    squares = jnp.sum((value * value).reshape(-1, 8, value.shape[1]), axis=0)
    out[rows:, :] = squares


def finish_kernel(groups, inner, outer, q_rows, k_rows, count, where, *refs):
    squares = refs[0]
    lines = refs[1 : 1 + groups * inner]
    gq_ref, gk_ref = refs[1 + groups * inner :]
    mean = jnp.sum(jnp.sum(squares[...], axis=0, keepdims=True), axis=1, keepdims=True) / count
    factor = 1.0 / jnp.sqrt(mean + EPSILON)
    total = outer * inner
    for g in range(groups):
        for e in range(inner):
            for f in range(outer):
                i = lax.rem(where[0] - f + outer, outer)
                j = lax.rem(where[1] - e + inner, inner)
                s = i * inner + j
                line = lines[g * inner + e]
                q_at = pl.multiple_of((g * total + s) * q_rows, q_rows)
                k_at = pl.multiple_of((g * total + s) * k_rows, k_rows)
                gq_ref[pl.ds(q_at, q_rows), :] = line[f, :q_rows, :] * factor
                gk_ref[pl.ds(k_at, k_rows), :] = line[f, q_rows : q_rows + k_rows, :] * factor


def butterfly(value, axis):
    size = lax.axis_size(axis)
    hop = 1
    while hop < size:
        value = value + ppermute(value, [(s, s ^ hop) for s in range(size)], axis)
        hop *= 2
    return value


def ppermute(value, pairs, axis="seq"):
    return lax.ppermute(value, axis, pairs)


def on_device(queries, key_heads, value_heads, query_map, key_map):
    heads = query_map.shape[0]
    groups, dh, feat = key_map.shape
    rows = queries.shape[0]
    ratio = heads // groups
    pair = 2 if ratio % 2 == 0 else 1
    total = lax.axis_size("seq")
    inner = 1 << ((total.bit_length() - 1) // 2)
    outer = total // inner
    me = lax.axis_index("seq")
    outer_me, inner_me = me // inner, me % inner
    at = lambda i, j: i * inner + j
    own = pl.pallas_call(
        pack_kernel,
        out_shape=jax.ShapeDtypeStruct((rows, 2 * groups * dh), F32),
        out_specs=pl.BlockSpec(memory_space=pltpu.VMEM),
        compiler_params=pltpu.CompilerParams(vmem_limit_bytes=LIMIT),
        name="pack",
    )(key_heads, value_heads)

    along, across = [], []
    moving = own
    for i in range(outer):
        if i > 0:
            pairs = [(at(p, j), at(p + 1, j)) for p in range(i - 1, outer - 1) for j in range(inner)]
            moving = ppermute(moving, pairs)
        along.append((moving, outer_me >= i))
        side = []
        last = i == outer - 1 and i > 0
        for d in range(1, inner):
            pairs = [
                (at(p, (j + d) % inner), at(p, j))
                for p in range(i, outer)
                for j in range(inner)
                if i > 0 or (j + d) % inner < j
            ]
            flag = outer_me >= i if i > 0 else (inner_me + d) % inner < inner_me
            if last and rows % 16 == 0:
                half = rows // 2
                ahead = across[i - 1][d - 1][0]
                line = [(at(i - 1, j), at(i, j)) for j in range(inner)]
                parts = [ppermute(moving[:half], pairs), ppermute(ahead[half:], line)]
                side.append((jnp.concatenate(parts, axis=0), flag))
            else:
                side.append((ppermute(moving, pairs), flag))
        across.append(side)

    always = jnp.ones((1,), jnp.int32)
    turned, stat, acc = attend(queries, [own], always, key_map, None, heads, 4)
    state = [stat, acc, jnp.zeros((groups, feat, dh), F32), jnp.zeros((groups, 8, feat), F32)]
    mine = local(queries, own, query_map, key_map, pair)
    blocks, flags, sigs = [], [], []
    for i in range(1, outer + 1):
        now = (along[i : i + 1] if i < outer else []) + across[i - 1]
        if now:
            here = [b for b, _ in now]
            on = jnp.stack([f.astype(jnp.int32) for _, f in now])
            *state, sig = attend(turned, here, on, key_map, state, heads, 4)
            sigs.append(sig)
            blocks += here
            flags.append(on)
    flags = jnp.concatenate(flags)

    total_heads = heads * lax.axis_size("head")
    cells = (total_heads + groups * lax.axis_size("head")) * dh * feat
    places = jnp.stack([outer_me, inner_me]).astype(jnp.int32)
    scalars = jnp.concatenate([flags, places])
    share = (ratio + 1) * dh // total
    sizes = (groups, heads, outer, inner, dh, feat)
    over = lambda d: [(at(p, j), at(p, (j + d) % inner)) for p in range(outer) for j in range(inner)]
    up = lambda d: [(at(p, j), at((p + d) % outer, j)) for p in range(outer) for j in range(inner)]
    vmem = pl.BlockSpec(memory_space=pltpu.VMEM)
    lines = []
    for g in range(groups):
        parts = learn(g, scalars, queries, own, state, mine, blocks, sigs, sizes, pair)
        taken = [ppermute(parts[d], over(d)) for d in range(1, inner)]
        half = [functools.reduce(jnp.add, [x[f] for x in taken], parts[0][f]) for f in range(outer)]
        taken = [ppermute(half[d], up(d)) for d in range(1, outer)]
        piece = pl.pallas_call(
            piece_kernel,
            out_shape=jax.ShapeDtypeStruct((share + 8, feat), F32),
            in_specs=[vmem] * outer,
            out_specs=vmem,
            compiler_params=pltpu.CompilerParams(vmem_limit_bytes=LIMIT),
        )(half[0], *taken)
        found = [piece] + [ppermute(piece, up(d)) for d in range(1, outer)]
        lines.append(jnp.stack(found))

    squares = sum(x[f, share:] for x in lines for f in range(outer))
    squares = butterfly(squares, "head")
    squares = functools.reduce(jnp.add, [ppermute(squares, over(d)) for d in range(1, inner)], squares)
    crossed = [[line] + [ppermute(line, over(d)) for d in range(1, inner)] for line in lines]
    crossed = [x for group in crossed for x in group]
    q_rows, k_rows = ratio * dh // total, dh // total
    gq, gk = pl.pallas_call(
        functools.partial(finish_kernel, groups, inner, outer, q_rows, k_rows, cells),
        out_shape=[
            jax.ShapeDtypeStruct((heads * dh, feat), F32),
            jax.ShapeDtypeStruct((groups * dh, feat), F32),
        ],
        in_specs=[pl.BlockSpec(memory_space=pltpu.SMEM)] + [vmem] * (1 + len(crossed)),
        compiler_params=pltpu.CompilerParams(vmem_limit_bytes=LIMIT),
        name="finish",
    )(places, squares, *crossed)
    return gq.reshape(heads, dh, feat), gk.reshape(groups, dh, feat)


def solution(mesh):
    placed = (
        P("seq", "head"),
        P("seq", "head"),
        P("seq", "head"),
        P("head", None, None),
        P("head", None, None),
    )

    return jax.shard_map(
        on_device,
        mesh=mesh,
        in_specs=placed,
        out_specs=(P("head", None, None), P("head", None, None)),
        check_vma=False,
    )
```

profile of v0, /device:TPU:0, one launch (start us, length us, event | category | flops | bytes accessed | tf_op | source)
XLA Modules:
  0.0 127.0 jit_solution(17256692353307696993)
XLA Ops:
  0.6 0.9 copy-done.2
  1.6 0.9 copy-done.3
  2.6 5.0 %collective-permute-start = (f32[256,512]{1,0:T(8,128)S(1)}, f32[256,512]{1,0:T(8,128)S(1)}, u32[]{:S(2)}, u32[]{:S(2)}) collective-permute-start(f32[256,512]{1,0:T(8,128)S(1)} %pack.1.refs_1_), channel_id=1, source_target_pairs={{0,8},{4,12},{8,16},{12,20},{16,24},{20,28},{1,9},{5,13},{9,17},{1... | collective-permute-start | bytes 1572872 | tf_op jit(solution)/shard_map/ppermute | solution.py:454
  7.6 3.4 %collective-permute-start.7 = (f32[256,512]{1,0:T(8,128)S(1)}, f32[256,512]{1,0:T(8,128)S(1)}, u32[]{:S(2)}, u32[]{:S(2)}) collective-permute-start(f32[256,512]{1,0:T(8,128)S(1)} %pack.1.refs_1_), channel_id=1, source_target_pairs={{0,4},{8,12},{16,20},{24,28},{1,5},{9,13},{17,21},{25,29},{2,6},{1... | collective-permute-start | bytes 1572872 | tf_op jit(solution)/shard_map/ppermute | solution.py:454
  11.4 1.6 %copy-done = f32[256,2048]{1,0:T(8,128)S(1)} copy-done((f32[256,2048]{1,0:T(8,128)S(1)}, f32[256,2048]{1,0:T(8,128)}, u32[]{:S(2)}) %copy-start) | copy-done | bytes 2097176
  13.0 3.8 %attend.5 = (bf16[16,256,256]{2,1,0:T(8,128)(2,1)S(1)}, f32[16,2,256]{2,1,0:T(2,128)S(1)}, f32[16,128,256]{2,1,0:T(8,128)S(1)}) custom-call(s32[1]{0:T(128)} %constant.40.clone.1.flags, f32[256,2048]{1,0:T(8,128)S(1)} %copy-done, f32[256,512]{1,0:T(8,128)S(1)} %pack.1.refs_1_), custom_call_target="tpu_custom_call" | custom-call | flops 3221225472 | bytes 6291456 | tf_op jit(solution)/shard_map/attend/pallas_call | solution.py:191
  16.8 6.8 %shard_map.68 = (bf16[16,256,256]{2,1,0:T(8,128)(2,1)S(1)}, f32[16,256,128]{2,1,0:T(8,128)S(1)}, f32[16,256,128]{2,1,0:T(8,128)S(1)}, f32[16,256,128]{2,1,0:T(8,...) custom-call(f32[256,2048]{1,0:T(8,128)S(1)} %copy-done.1, f32[256,512]{1,0:T(8,128)S(1)} %pack.1.refs_1_, ...), custom_call_target="tpu_custom_call" | custom-call | flops 3221225472 | bytes 4194304 | tf_op jit(solution)/shard_map/pallas_call | solution.py:258
  27.1 0.7 attend.7
  29.9 5.7 %shard_map.69 = (f32[4,144,128]{2,1,0:T(8,128)S(1)}, f32[4,144,128]{2,1,0:T(8,128)S(1)}) custom-call(s32[9]{0:T(128)S(1)} %concatenate.7.flags, f32[256,2048]{1,0:T(8,128)S(1)} %copy-done.1, f32[256,512]{1,0:T(8,128)S(1)} %pack.1.refs_1_, f32[2,128,128]{2,1,0:T(8,128)S(1)} %get-tuple-element.52.refs_2_, f32[2,8,128]{2,1,0:T(8,128)S(1)} %get-tuple-element.53.refs_3_, ...), custom_call_target="tpu_custom_call" | custom-call | flops 2684354560 | bytes 4194304 | tf_op jit(solution)/shard_map/pallas_call | solution.py:258
  35.7 3.6 %collective-permute-start.8 = (f32[4,144,128]{2,1,0:T(8,128)S(1)}, f32[4,144,128]{2,1,0:T(8,128)S(1)}, u32[]{:S(2)}, u32[]{:S(2)}) collective-permute-start(f32[4,144,128]{2,1,0:T(8,128)S(1)} %get-tuple-element.67), channel_id=1, source_target_pairs={{0,4},{4,0},{8,12},{12,8},{16,20},{20,16},{24,28},{28,24},{1,5},{5... | collective-permute-start | bytes 884744 | tf_op jit(solution)/shard_map/ppermute | solution.py:454
  39.2 5.7 %shard_map.71 = (f32[4,144,128]{2,1,0:T(8,128)S(1)}, f32[4,144,128]{2,1,0:T(8,128)S(1)}) custom-call(s32[9]{0:T(128)S(1)} %concatenate.7.flags, f32[256,2048]{1,0:T(8,128)S(1)} %copy-done.1, f32[256,512]{1,0:T(8,128)S(1)} %pack.1.refs_1_, f32[2,128,128]{2,1,0:T(8,128)S(1)} %get-tuple-element.52.refs_2_, f32[2,8,128]{2,1,0:T(8,128)S(1)} %get-tuple-element.53.refs_3_, ...), custom_call_target="tpu_custom_call" | custom-call | flops 2684354560 | bytes 4194304 | tf_op jit(solution)/shard_map/pallas_call | solution.py:258
  45.0 1.0 collective-permute-done.8
  46.0 18.1 %collective-permute-start.9 = (f32[144,128]{1,0:T(8,128)S(1)}, f32[144,128]{1,0:T(8,128)S(1)}, u32[]{:S(2)}, u32[]{:S(2)}) collective-permute-start(f32[144,128]{1,0:T(8,128)S(1)} %get-tuple-element.74), channel_id=1, source_target_pairs={{0,8},{4,12},{8,16},{12,20},{16,24},{20,28},{24,0},{28,4},{1,9},{5... | collective-permute-start | bytes 221192 | tf_op jit(solution)/shard_map/ppermute | solution.py:454
  64.1 20.6 %collective-permute-start.10 = (f32[144,128]{1,0:T(8,128)S(1)}, f32[144,128]{1,0:T(8,128)S(1)}, u32[]{:S(2)}, u32[]{:S(2)}) collective-permute-start(f32[144,128]{1,0:T(8,128)S(1)} %get-tuple-element.73), channel_id=1, source_target_pairs={{0,16},{4,20},{8,24},{12,28},{16,0},{20,4},{24,8},{28,12},{1,17},{... | collective-permute-start | bytes 221192 | tf_op jit(solution)/shard_map/ppermute | solution.py:454
  84.7 2.1 %collective-permute-start.16 = (f32[144,128]{1,0:T(8,128)S(1)}, f32[144,128]{1,0:T(8,128)S(1)}, u32[]{:S(2)}, u32[]{:S(2)}) collective-permute-start(f32[144,128]{1,0:T(8,128)S(1)} %get-tuple-element.78), channel_id=1, source_target_pairs={{0,8},{4,12},{8,16},{12,20},{16,24},{20,28},{24,0},{28,4},{1,9},{5... | collective-permute-start | bytes 221192 | tf_op jit(solution)/shard_map/ppermute | solution.py:454
  86.8 1.5 %collective-permute-done.10.refs_2_ = f32[144,128]{1,0:T(8,128)S(1)} collective-permute-done((f32[144,128]{1,0:T(8,128)S(1)}, f32[144,128]{1,0:T(8,128)S(1)}, u32[]{:S(2)}, u32[]{:S(2)}) %collective-permute-start.10) | collective-permute-done | bytes 73760 | tf_op jit(solution)/shard_map/ppermute | solution.py:454
  88.3 2.1 %collective-permute-done.11.refs_3_ = f32[144,128]{1,0:T(8,128)S(1)} collective-permute-done((f32[144,128]{1,0:T(8,128)S(1)}, f32[144,128]{1,0:T(8,128)S(1)}, u32[]{:S(2)}, u32[]{:S(2)}) %collective-permute-start.11) | collective-permute-done | bytes 73760 | tf_op jit(solution)/shard_map/ppermute | solution.py:454
  90.4 1.3 %collective-permute-start.14 = (f32[152,128]{1,0:T(8,128)S(1)}, f32[152,128]{1,0:T(8,128)S(1)}, u32[]{:S(2)}, u32[]{:S(2)}) collective-permute-start(f32[152,128]{1,0:T(8,128)S(1)} %shard_map.70), channel_id=1, source_target_pairs={{0,24},{4,28},{8,0},{12,4},{16,8},{20,12},{24,16},{28,20},{1,25},{... | collective-permute-start | bytes 233480 | tf_op jit(solution)/shard_map/ppermute | solution.py:454
  91.8 1.6 %collective-permute-start.13 = (f32[152,128]{1,0:T(8,128)S(1)}, f32[152,128]{1,0:T(8,128)S(1)}, u32[]{:S(2)}, u32[]{:S(2)}) collective-permute-start(f32[152,128]{1,0:T(8,128)S(1)} %shard_map.70), channel_id=1, source_target_pairs={{0,16},{4,20},{8,24},{12,28},{16,0},{20,4},{24,8},{28,12},{1,17},{... | collective-permute-start | bytes 233480 | tf_op jit(solution)/shard_map/ppermute | solution.py:454
  93.5 2.0 %collective-permute-start.17 = (f32[144,128]{1,0:T(8,128)S(1)}, f32[144,128]{1,0:T(8,128)S(1)}, u32[]{:S(2)}, u32[]{:S(2)}) collective-permute-start(f32[144,128]{1,0:T(8,128)S(1)} %get-tuple-element.77), channel_id=1, source_target_pairs={{0,16},{4,20},{8,24},{12,28},{16,0},{20,4},{24,8},{28,12},{1,17},{... | collective-permute-start | bytes 221192 | tf_op jit(solution)/shard_map/ppermute | solution.py:454
  95.4 2.2 %collective-permute-start.18 = (f32[144,128]{1,0:T(8,128)S(1)}, f32[144,128]{1,0:T(8,128)S(1)}, u32[]{:S(2)}, u32[]{:S(2)}) collective-permute-start(f32[144,128]{1,0:T(8,128)S(1)} %get-tuple-element.76), channel_id=1, source_target_pairs={{0,24},{4,28},{8,0},{12,4},{16,8},{20,12},{24,16},{28,20},{1,25},{... | collective-permute-start | bytes 221192 | tf_op jit(solution)/shard_map/ppermute | solution.py:454
  97.6 3.5 %collective-permute-done.17.refs_2_ = f32[144,128]{1,0:T(8,128)S(1)} collective-permute-done((f32[144,128]{1,0:T(8,128)S(1)}, f32[144,128]{1,0:T(8,128)S(1)}, u32[]{:S(2)}, u32[]{:S(2)}) %collective-permute-start.17) | collective-permute-done | bytes 73760 | tf_op jit(solution)/shard_map/ppermute | solution.py:454
  101.8 2.1 %collective-permute-start.21 = (f32[152,128]{1,0:T(8,128)S(1)}, f32[152,128]{1,0:T(8,128)S(1)}, u32[]{:S(2)}, u32[]{:S(2)}) collective-permute-start(f32[152,128]{1,0:T(8,128)S(1)} %shard_map.72), channel_id=1, source_target_pairs={{0,24},{4,28},{8,0},{12,4},{16,8},{20,12},{24,16},{28,20},{1,25},{... | collective-permute-start | bytes 233480 | tf_op jit(solution)/shard_map/ppermute | solution.py:454
  103.9 1.7 %collective-permute-start.20 = (f32[152,128]{1,0:T(8,128)S(1)}, f32[152,128]{1,0:T(8,128)S(1)}, u32[]{:S(2)}, u32[]{:S(2)}) collective-permute-start(f32[152,128]{1,0:T(8,128)S(1)} %shard_map.72), channel_id=1, source_target_pairs={{0,16},{4,20},{8,24},{12,28},{16,0},{20,4},{24,8},{28,12},{1,17},{... | collective-permute-start | bytes 233480 | tf_op jit(solution)/shard_map/ppermute | solution.py:454
  105.6 5.0 %collective-permute-start.25 = (f32[4,152,128]{2,1,0:T(8,128)S(1)}, f32[4,152,128]{2,1,0:T(8,128)S(1)}, u32[]{:S(2)}, u32[]{:S(2)}) collective-permute-start(f32[4,152,128]{2,1,0:T(8,128)S(1)} %pad_maximum_fusion.refs_1_), channel_id=1, source_target_pairs={{0,4},{4,0},{8,12},{12,8},{16,20},{20,16},{24,28},{28,24},{1,5},{5... | collective-permute-start | bytes 933896 | tf_op jit(solution)/shard_map/ppermute | solution.py:454
  110.7 1.1 collective-permute-done.19
  111.8 5.0 %collective-permute-start.26 = (f32[4,152,128]{2,1,0:T(8,128)S(1)}, f32[4,152,128]{2,1,0:T(8,128)S(1)}, u32[]{:S(2)}, u32[]{:S(2)}) collective-permute-start(f32[4,152,128]{2,1,0:T(8,128)S(1)} %pad_maximum_fusion.1.refs_3_), channel_id=1, source_target_pairs={{0,4},{4,0},{8,12},{12,8},{16,20},{20,16},{24,28},{28,24},{1,5},{5... | collective-permute-start | bytes 933896 | tf_op jit(solution)/shard_map/ppermute | solution.py:454
  116.9 1.2 collective-permute-done.22
  118.0 1.5 %collective-permute-start.23 = (f32[8,128]{1,0:T(8,128)S(1)}, f32[8,128]{1,0:T(8,128)S(1)}, u32[]{:S(2)}, u32[]{:S(2)}) collective-permute-start(f32[8,128]{1,0:T(8,128)S(1)} %add.120), channel_id=1, source_target_pairs={{0,2},{1,3},{2,0},{3,1},{4,6},{5,7},{6,4},{7,5},{8,10},{9,11},{10,... | collective-permute-start | bytes 12296 | tf_op jit(solution)/shard_map/ppermute | solution.py:454
  119.6 2.1 %collective-permute-done.23 = f32[8,128]{1,0:T(8,128)S(1)} collective-permute-done((f32[8,128]{1,0:T(8,128)S(1)}, f32[8,128]{1,0:T(8,128)S(1)}, u32[]{:S(2)}, u32[]{:S(2)}) %collective-permute-start.23) | collective-permute-done | bytes 4128 | tf_op jit(solution)/shard_map/ppermute | solution.py:454
  121.7 3.5 %collective-permute-done.24 = f32[8,128]{1,0:T(8,128)S(1)} collective-permute-done((f32[8,128]{1,0:T(8,128)S(1)}, f32[8,128]{1,0:T(8,128)S(1)}, u32[]{:S(2)}, u32[]{:S(2)}) %collective-permute-start.24) | collective-permute-done | bytes 4128 | tf_op jit(solution)/shard_map/ppermute | solution.py:454
  125.3 1.7 %finish.1 = (f32[2048,128]{1,0:T(8,128)}, f32[256,128]{1,0:T(8,128)}) custom-call(s32[2]{0:T(128)S(1)} %pad_add_fusion.where, f32[8,128]{1,0:T(8,128)S(1)} %add.122.refs_0_, f32[4,152,128]{2,1,0:T(8,128)S(1)} %pad_maximum_fusion.refs_1_, f32[4,152,128]{2,1,0:T(8,128)S(1)} %collective-permute-done.25.refs_2_, f32[4,152,128]{2,1,0:T(8,128)S(1)} %pad_maximum_fusion.1.refs_3_, ...), custom_call_target="tpu_custom_call" | custom-call | tf_op jit(solution)/shard_map/finish/pallas_call | solution.py:551
  (65 shorter events, 7.0 us)
Async XLA Ops:
  0.6 1.0 copy-start.2
  2.6 21.0 %collective-permute-start = (f32[256,512]{1,0:T(8,128)S(1)}, f32[256,512]{1,0:T(8,128)S(1)}, u32[]{:S(2)}, u32[]{:S(2)}) collective-permute-start(f32[256,512]{1,0:T(8,128)S(1)} %pack.1.refs_1_), channel_id=1, source_target_pairs={{0,8},{4,12},{8,16},{12,20},{16,24},{20,28},{1,9},{5,13},{9,17},{1... | collective-permute-start | bytes 1572872 | tf_op jit(solution)/shard_map/ppermute | solution.py:454
  7.6 17.5 %collective-permute-start.7 = (f32[256,512]{1,0:T(8,128)S(1)}, f32[256,512]{1,0:T(8,128)S(1)}, u32[]{:S(2)}, u32[]{:S(2)}) collective-permute-start(f32[256,512]{1,0:T(8,128)S(1)} %pack.1.refs_1_), channel_id=1, source_target_pairs={{0,4},{8,12},{16,20},{24,28},{1,5},{9,13},{17,21},{25,29},{2,6},{1... | collective-permute-start | bytes 1572872 | tf_op jit(solution)/shard_map/ppermute | solution.py:454
  11.4 1.6 %copy-start = (f32[256,2048]{1,0:T(8,128)S(1)}, f32[256,2048]{1,0:T(8,128)}, u32[]{:S(2)}) copy-start(f32[256,2048]{1,0:T(8,128)} %refs_0_.7) | copy-start | bytes 6291460
  13.0 3.8 %copy-start.1 = (f32[256,2048]{1,0:T(8,128)S(1)}, f32[256,2048]{1,0:T(8,128)}, u32[]{:S(2)}) copy-start(f32[256,2048]{1,0:T(8,128)} %refs_0_.7) | copy-start | bytes 6291460
  13.0 3.8 %copy-start.4 = (f32[16,128,128]{2,1,0:T(8,128)S(1)}, f32[16,128,128]{2,1,0:T(8,128)}, u32[]{:S(2)}) copy-start(f32[16,128,128]{2,1,0:T(8,128)} %refs_2_.3) | copy-start | bytes 3145732
  13.0 3.8 %copy-start.5 = (f32[2,128,128]{2,1,0:T(8,128)S(1)}, f32[2,128,128]{2,1,0:T(8,128)}, u32[]{:S(2)}) copy-start(f32[2,128,128]{2,1,0:T(8,128)} %refs_3_.7) | copy-start | bytes 393220
  23.6 2.0 %collective-permute-start.1 = (f32[256,512]{1,0:T(8,128)S(1)}, f32[256,512]{1,0:T(8,128)S(1)}, u32[]{:S(2)}, u32[]{:S(2)}) collective-permute-start(f32[256,512]{1,0:T(8,128)S(1)} %collective-permute-done.refs_1_.refs_12_), channel_id=1, source_target_pairs={{8,16},{12,20},{16,24},{20,28},{9,17},{13,21},{17,25},{21,29},{10,... | collective-permute-start | bytes 1572872 | tf_op jit(solution)/shard_map/ppermute | solution.py:454
  24.3 2.7 %collective-permute-start.6 = (f32[256,512]{1,0:T(8,128)S(1)}, f32[256,512]{1,0:T(8,128)S(1)}, u32[]{:S(2)}, u32[]{:S(2)}) collective-permute-start(f32[256,512]{1,0:T(8,128)S(1)} %collective-permute-done.refs_1_.refs_12_), channel_id=1, source_target_pairs={{12,8},{8,12},{20,16},{16,20},{28,24},{24,28},{13,9},{9,13},{21,17... | collective-permute-start | bytes 1572872 | tf_op jit(solution)/shard_map/ppermute | solution.py:454
  25.6 2.2 %collective-permute-start.2 = (f32[256,512]{1,0:T(8,128)S(1)}, f32[256,512]{1,0:T(8,128)S(1)}, u32[]{:S(2)}, u32[]{:S(2)}) collective-permute-start(f32[256,512]{1,0:T(8,128)S(1)} %collective-permute-done.1.refs_1_.refs_14_), channel_id=1, source_target_pairs={{16,24},{20,28},{17,25},{21,29},{18,26},{22,30},{19,27},{23,31}} | collective-permute-start | bytes 1572872 | tf_op jit(solution)/shard_map/ppermute | solution.py:454
  26.4 2.2 %collective-permute-start.4 = (f32[256,512]{1,0:T(8,128)S(1)}, f32[256,512]{1,0:T(8,128)S(1)}, u32[]{:S(2)}, u32[]{:S(2)}) collective-permute-start(f32[256,512]{1,0:T(8,128)S(1)} %collective-permute-done.1.refs_1_.refs_14_), channel_id=1, source_target_pairs={{20,16},{16,20},{28,24},{24,28},{21,17},{17,21},{29,25},{25,29},{2... | collective-permute-start | bytes 1572872 | tf_op jit(solution)/shard_map/ppermute | solution.py:454
  27.9 2.0 %collective-permute-start.3 = (f32[128,512]{1,0:T(8,128)S(1)}, f32[128,512]{1,0:T(8,128)S(1)}, u32[]{:S(2)}, u32[]{:S(2)}) collective-permute-start(f32[128,512]{1,0:T(8,128)S(1)} %slice.104), channel_id=1, source_target_pairs={{28,24},{24,28},{29,25},{25,29},{30,26},{26,30},{31,27},{27,31}} | collective-permute-start | bytes 786440 | tf_op jit(solution)/shard_map/ppermute | solution.py:454
  28.6 1.3 %collective-permute-start.5 = (f32[128,512]{1,0:T(8,128)S(1)}, f32[128,512]{1,0:T(8,128)S(1)}, u32[]{:S(2)}, u32[]{:S(2)}) collective-permute-start(f32[128,512]{1,0:T(8,128)S(1)} %slice.105), channel_id=1, source_target_pairs={{16,24},{20,28},{17,25},{21,29},{18,26},{22,30},{19,27},{23,31}} | collective-permute-start | bytes 786440 | tf_op jit(solution)/shard_map/ppermute | solution.py:454
  35.7 10.3 %collective-permute-start.8 = (f32[4,144,128]{2,1,0:T(8,128)S(1)}, f32[4,144,128]{2,1,0:T(8,128)S(1)}, u32[]{:S(2)}, u32[]{:S(2)}) collective-permute-start(f32[4,144,128]{2,1,0:T(8,128)S(1)} %get-tuple-element.67), channel_id=1, source_target_pairs={{0,4},{4,0},{8,12},{12,8},{16,20},{20,16},{24,28},{28,24},{1,5},{5... | collective-permute-start | bytes 884744 | tf_op jit(solution)/shard_map/ppermute | solution.py:454
  44.9 39.8 %collective-permute-start.15 = (f32[4,144,128]{2,1,0:T(8,128)S(1)}, f32[4,144,128]{2,1,0:T(8,128)S(1)}, u32[]{:S(2)}, u32[]{:S(2)}) collective-permute-start(f32[4,144,128]{2,1,0:T(8,128)S(1)} %get-tuple-element.69), channel_id=1, source_target_pairs={{0,4},{4,0},{8,12},{12,8},{16,20},{20,16},{24,28},{28,24},{1,5},{5... | collective-permute-start | bytes 884744 | tf_op jit(solution)/shard_map/ppermute | solution.py:454
  46.0 40.8 %collective-permute-start.9 = (f32[144,128]{1,0:T(8,128)S(1)}, f32[144,128]{1,0:T(8,128)S(1)}, u32[]{:S(2)}, u32[]{:S(2)}) collective-permute-start(f32[144,128]{1,0:T(8,128)S(1)} %get-tuple-element.74), channel_id=1, source_target_pairs={{0,8},{4,12},{8,16},{12,20},{16,24},{20,28},{24,0},{28,4},{1,9},{5... | collective-permute-start | bytes 221192 | tf_op jit(solution)/shard_map/ppermute | solution.py:454
  64.1 24.2 %collective-permute-start.10 = (f32[144,128]{1,0:T(8,128)S(1)}, f32[144,128]{1,0:T(8,128)S(1)}, u32[]{:S(2)}, u32[]{:S(2)}) collective-permute-start(f32[144,128]{1,0:T(8,128)S(1)} %get-tuple-element.73), channel_id=1, source_target_pairs={{0,16},{4,20},{8,24},{12,28},{16,0},{20,4},{24,8},{28,12},{1,17},{... | collective-permute-start | bytes 221192 | tf_op jit(solution)/shard_map/ppermute | solution.py:454
  84.7 5.7 %collective-permute-start.11 = (f32[144,128]{1,0:T(8,128)S(1)}, f32[144,128]{1,0:T(8,128)S(1)}, u32[]{:S(2)}, u32[]{:S(2)}) collective-permute-start(f32[144,128]{1,0:T(8,128)S(1)} %get-tuple-element.72), channel_id=1, source_target_pairs={{0,24},{4,28},{8,0},{12,4},{16,8},{20,12},{24,16},{28,20},{1,25},{... | collective-permute-start | bytes 221192 | tf_op jit(solution)/shard_map/ppermute | solution.py:454
  84.7 10.7 %collective-permute-start.16 = (f32[144,128]{1,0:T(8,128)S(1)}, f32[144,128]{1,0:T(8,128)S(1)}, u32[]{:S(2)}, u32[]{:S(2)}) collective-permute-start(f32[144,128]{1,0:T(8,128)S(1)} %get-tuple-element.78), channel_id=1, source_target_pairs={{0,8},{4,12},{8,16},{12,20},{16,24},{20,28},{24,0},{28,4},{1,9},{5... | collective-permute-start | bytes 221192 | tf_op jit(solution)/shard_map/ppermute | solution.py:454
  90.4 15.1 %collective-permute-start.14 = (f32[152,128]{1,0:T(8,128)S(1)}, f32[152,128]{1,0:T(8,128)S(1)}, u32[]{:S(2)}, u32[]{:S(2)}) collective-permute-start(f32[152,128]{1,0:T(8,128)S(1)} %shard_map.70), channel_id=1, source_target_pairs={{0,24},{4,28},{8,0},{12,4},{16,8},{20,12},{24,16},{28,20},{1,25},{... | collective-permute-start | bytes 233480 | tf_op jit(solution)/shard_map/ppermute | solution.py:454
  91.8 13.8 %collective-permute-start.13 = (f32[152,128]{1,0:T(8,128)S(1)}, f32[152,128]{1,0:T(8,128)S(1)}, u32[]{:S(2)}, u32[]{:S(2)}) collective-permute-start(f32[152,128]{1,0:T(8,128)S(1)} %shard_map.70), channel_id=1, source_target_pairs={{0,16},{4,20},{8,24},{12,28},{16,0},{20,4},{24,8},{28,12},{1,17},{... | collective-permute-start | bytes 233480 | tf_op jit(solution)/shard_map/ppermute | solution.py:454
  93.4 12.2 %collective-permute-start.12 = (f32[152,128]{1,0:T(8,128)S(1)}, f32[152,128]{1,0:T(8,128)S(1)}, u32[]{:S(2)}, u32[]{:S(2)}) collective-permute-start(f32[152,128]{1,0:T(8,128)S(1)} %shard_map.70), channel_id=1, source_target_pairs={{0,8},{4,12},{8,16},{12,20},{16,24},{20,28},{24,0},{28,4},{1,9},{5... | collective-permute-start | bytes 233480 | tf_op jit(solution)/shard_map/ppermute | solution.py:454
  93.5 7.7 %collective-permute-start.17 = (f32[144,128]{1,0:T(8,128)S(1)}, f32[144,128]{1,0:T(8,128)S(1)}, u32[]{:S(2)}, u32[]{:S(2)}) collective-permute-start(f32[144,128]{1,0:T(8,128)S(1)} %get-tuple-element.77), channel_id=1, source_target_pairs={{0,16},{4,20},{8,24},{12,28},{16,0},{20,4},{24,8},{28,12},{1,17},{... | collective-permute-start | bytes 221192 | tf_op jit(solution)/shard_map/ppermute | solution.py:454
  95.4 6.3 %collective-permute-start.18 = (f32[144,128]{1,0:T(8,128)S(1)}, f32[144,128]{1,0:T(8,128)S(1)}, u32[]{:S(2)}, u32[]{:S(2)}) collective-permute-start(f32[144,128]{1,0:T(8,128)S(1)} %get-tuple-element.76), channel_id=1, source_target_pairs={{0,24},{4,28},{8,0},{12,4},{16,8},{20,12},{24,16},{28,20},{1,25},{... | collective-permute-start | bytes 221192 | tf_op jit(solution)/shard_map/ppermute | solution.py:454
  101.8 8.9 %collective-permute-start.21 = (f32[152,128]{1,0:T(8,128)S(1)}, f32[152,128]{1,0:T(8,128)S(1)}, u32[]{:S(2)}, u32[]{:S(2)}) collective-permute-start(f32[152,128]{1,0:T(8,128)S(1)} %shard_map.72), channel_id=1, source_target_pairs={{0,24},{4,28},{8,0},{12,4},{16,8},{20,12},{24,16},{28,20},{1,25},{... | collective-permute-start | bytes 233480 | tf_op jit(solution)/shard_map/ppermute | solution.py:454
  103.9 6.8 %collective-permute-start.20 = (f32[152,128]{1,0:T(8,128)S(1)}, f32[152,128]{1,0:T(8,128)S(1)}, u32[]{:S(2)}, u32[]{:S(2)}) collective-permute-start(f32[152,128]{1,0:T(8,128)S(1)} %shard_map.72), channel_id=1, source_target_pairs={{0,16},{4,20},{8,24},{12,28},{16,0},{20,4},{24,8},{28,12},{1,17},{... | collective-permute-start | bytes 233480 | tf_op jit(solution)/shard_map/ppermute | solution.py:454
  105.6 6.2 %collective-permute-start.19 = (f32[152,128]{1,0:T(8,128)S(1)}, f32[152,128]{1,0:T(8,128)S(1)}, u32[]{:S(2)}, u32[]{:S(2)}) collective-permute-start(f32[152,128]{1,0:T(8,128)S(1)} %shard_map.72), channel_id=1, source_target_pairs={{0,8},{4,12},{8,16},{12,20},{16,24},{20,28},{24,0},{28,4},{1,9},{5... | collective-permute-start | bytes 233480 | tf_op jit(solution)/shard_map/ppermute | solution.py:454
  105.6 19.6 %collective-permute-start.25 = (f32[4,152,128]{2,1,0:T(8,128)S(1)}, f32[4,152,128]{2,1,0:T(8,128)S(1)}, u32[]{:S(2)}, u32[]{:S(2)}) collective-permute-start(f32[4,152,128]{2,1,0:T(8,128)S(1)} %pad_maximum_fusion.refs_1_), channel_id=1, source_target_pairs={{0,4},{4,0},{8,12},{12,8},{16,20},{20,16},{24,28},{28,24},{1,5},{5... | collective-permute-start | bytes 933896 | tf_op jit(solution)/shard_map/ppermute | solution.py:454
  111.8 13.5 %collective-permute-start.26 = (f32[4,152,128]{2,1,0:T(8,128)S(1)}, f32[4,152,128]{2,1,0:T(8,128)S(1)}, u32[]{:S(2)}, u32[]{:S(2)}) collective-permute-start(f32[4,152,128]{2,1,0:T(8,128)S(1)} %pad_maximum_fusion.1.refs_3_), channel_id=1, source_target_pairs={{0,4},{4,0},{8,12},{12,8},{16,20},{20,16},{24,28},{28,24},{1,5},{5... | collective-permute-start | bytes 933896 | tf_op jit(solution)/shard_map/ppermute | solution.py:454
  116.8 1.2 collective-permute-start.22
  118.0 3.6 %collective-permute-start.23 = (f32[8,128]{1,0:T(8,128)S(1)}, f32[8,128]{1,0:T(8,128)S(1)}, u32[]{:S(2)}, u32[]{:S(2)}) collective-permute-start(f32[8,128]{1,0:T(8,128)S(1)} %add.120), channel_id=1, source_target_pairs={{0,2},{1,3},{2,0},{3,1},{4,6},{5,7},{6,4},{7,5},{8,10},{9,11},{10,... | collective-permute-start | bytes 12296 | tf_op jit(solution)/shard_map/ppermute | solution.py:454
  121.6 3.6 %collective-permute-start.24 = (f32[8,128]{1,0:T(8,128)S(1)}, f32[8,128]{1,0:T(8,128)S(1)}, u32[]{:S(2)}, u32[]{:S(2)}) collective-permute-start(f32[8,128]{1,0:T(8,128)S(1)} %add.121), channel_id=1, source_target_pairs={{0,4},{4,0},{8,12},{12,8},{16,20},{20,16},{24,28},{28,24},{1,5},{5... | collective-permute-start | bytes 12296 | tf_op jit(solution)/shard_map/ppermute | solution.py:454
  (1 other events, 0.9 us)
where the time goes:
time: 127 us
  starting transfers between devices  79.5 us (63%)
  Pallas kernels  25.7 us (20%)
  waiting for transfers between devices  16.6 us (13%)
  local copies, waits for them, and re-layouts  3.67 us (3%)
    ppermute x27, starting transfers between devices, ppermute(): return lax.ppermute(value, axis, pairs)  79.5 us
    pallas_call x3, Pallas kernels, vmem_call(): pl.pallas_call(kernel, out_shape=out_shape, in_specs=([smem] if first_sme...  18.2 us
    ppermute x27, waiting for transfers between devices, ppermute(): return lax.ppermute(value, axis, pairs)  16.6 us
    pallas_call x5, Pallas kernels, attend(): pl.pallas_call(functools.partial(attend_kernel, first, count, groups, pai...  5.71 us
    unnamed x13, local copies, waits for them, and re-layouts  3.52 us
  transfers between devices with their start and end apart: 27, of which 9 were waited for; matrix products, arithmetic and copies ran while one was open for 0% of the time, Pallas kernels for 14%

commit v1 on v0

--- a/solution.py
+++ b/solution.py
@@ -478,7 +478,7 @@
     moving = own
     for i in range(outer):
         if i > 0:
-            pairs = [(at(p, j), at(p + 1, j)) for p in range(i - 1, outer - 1) for j in range(inner)]
+            pairs = [(at(p, j), at(p + 1, j)) for p in range(outer - 1) for j in range(inner)]
             moving = ppermute(moving, pairs)
         along.append((moving, outer_me >= i))
         side = []
@@ -486,15 +486,14 @@
         for d in range(1, inner):
             pairs = [
                 (at(p, (j + d) % inner), at(p, j))
-                for p in range(i, outer)
+                for p in range(outer)
                 for j in range(inner)
-                if i > 0 or (j + d) % inner < j
             ]
             flag = outer_me >= i if i > 0 else (inner_me + d) % inner < inner_me
             if last and rows % 16 == 0:
                 half = rows // 2
                 ahead = across[i - 1][d - 1][0]
-                line = [(at(i - 1, j), at(i, j)) for j in range(inner)]
+                line = [(at(p, j), at(p + 1, j)) for p in range(outer - 1) for j in range(inner)]
                 parts = [ppermute(moving[:half], pairs), ppermute(ahead[half:], line)]
                 side.append((jnp.concatenate(parts, axis=0), flag))
             else:

time: 127 us -> 123 us (0.969)
  starting transfers between devices: 79.5 us -> 50.1 us
  waiting for transfers between devices: 16.6 us -> 41.9 us
    ppermute x27, starting transfers between devices: 79.5 us -> 50.1 us  [ppermute(): return lax.ppermute(value, axis, pairs)]
    ppermute x27, waiting for transfers between devices: 16.6 us -> 41.9 us  [ppermute(): return lax.ppermute(value, axis, pairs)]
  transfers between devices with their start and end apart: 27 -> 27, of which waited for: 9 -> 14; matrix products, arithmetic and copies ran while one was open for 0% -> 1% of each run, Pallas kernels for 14% -> 15%
where the time goes in v1:
time: 123 us
  starting transfers between devices  50.1 us (41%)
  waiting for transfers between devices  41.9 us (34%)
  Pallas kernels  25.7 us (21%)
  local copies, waits for them, and re-layouts  3.67 us (3%)
    ppermute x27, starting transfers between devices, ppermute(): return lax.ppermute(value, axis, pairs)  50.1 us
    ppermute x27, waiting for transfers between devices, ppermute(): return lax.ppermute(value, axis, pairs)  41.9 us
    pallas_call x3, Pallas kernels, vmem_call(): pl.pallas_call(kernel, out_shape=out_shape, in_specs=([smem] if first_sme...  18.2 us
    pallas_call x5, Pallas kernels, attend(): pl.pallas_call(functools.partial(attend_kernel, first, count, groups, pai...  5.71 us
    unnamed x13, local copies, waits for them, and re-layouts  3.52 us
  transfers between devices with their start and end apart: 27, of which 14 were waited for; matrix products, arithmetic and copies ran while one was open for 1% of the time, Pallas kernels for 15%

profile of v1, /device:TPU:0, one launch (start us, length us, event | category | flops | bytes accessed | tf_op | source)
XLA Modules:
  0.0 122.8 jit_solution(18276994299028006303)
XLA Ops:
  2.6 5.0 %collective-permute-start = (f32[256,512]{1,0:T(8,128)S(1)}, f32[256,512]{1,0:T(8,128)S(1)}, u32[]{:S(2)}, u32[]{:S(2)}) collective-permute-start(f32[256,512]{1,0:T(8,128)S(1)} %pack.1.refs_1_), channel_id=1, source_target_pairs={{0,8},{4,12},{8,16},{12,20},{16,24},{20,28},{1,9},{5,13},{9,17},{1... | collective-permute-start | bytes 1572872 | tf_op jit(solution)/shard_map/ppermute | solution.py:454
  7.6 1.6 %collective-permute-start.7 = (f32[256,512]{1,0:T(8,128)S(1)}, f32[256,512]{1,0:T(8,128)S(1)}, u32[]{:S(2)}, u32[]{:S(2)}) collective-permute-start(f32[256,512]{1,0:T(8,128)S(1)} %pack.1.refs_1_), channel_id=1, source_target_pairs={{4,0},{0,4},{12,8},{8,12},{20,16},{16,20},{28,24},{24,28},{5,1},{1... | collective-permute-start | bytes 1572872 | tf_op jit(solution)/shard_map/ppermute | solution.py:454
  9.4 1.6 %copy-done = f32[256,2048]{1,0:T(8,128)S(1)} copy-done((f32[256,2048]{1,0:T(8,128)S(1)}, f32[256,2048]{1,0:T(8,128)}, u32[]{:S(2)}) %copy-start) | copy-done | bytes 2097176
  11.0 3.8 %attend.5 = (bf16[16,256,256]{2,1,0:T(8,128)(2,1)S(1)}, f32[16,2,256]{2,1,0:T(2,128)S(1)}, f32[16,128,256]{2,1,0:T(8,128)S(1)}) custom-call(s32[1]{0:T(128)} %constant.40.clone.1.flags, f32[256,2048]{1,0:T(8,128)S(1)} %copy-done, f32[256,512]{1,0:T(8,128)S(1)} %pack.1.refs_1_), custom_call_target="tpu_custom_call" | custom-call | flops 3221225472 | bytes 6291456 | tf_op jit(solution)/shard_map/attend/pallas_call | solution.py:191
  14.9 6.8 %shard_map.68 = (bf16[16,256,256]{2,1,0:T(8,128)(2,1)S(1)}, f32[16,256,128]{2,1,0:T(8,128)S(1)}, f32[16,256,128]{2,1,0:T(8,128)S(1)}, f32[16,256,128]{2,1,0:T(8,...) custom-call(f32[256,2048]{1,0:T(8,128)S(1)} %copy-done.1, f32[256,512]{1,0:T(8,128)S(1)} %pack.1.refs_1_, ...), custom_call_target="tpu_custom_call" | custom-call | flops 3221225472 | bytes 4194304 | tf_op jit(solution)/shard_map/pallas_call | solution.py:258
  21.7 3.5 %collective-permute-start.1 = (f32[256,512]{1,0:T(8,128)S(1)}, f32[256,512]{1,0:T(8,128)S(1)}, u32[]{:S(2)}, u32[]{:S(2)}) collective-permute-start(f32[256,512]{1,0:T(8,128)S(1)} %collective-permute-done.refs_1_.refs_12_), channel_id=1, source_target_pairs={{0,8},{4,12},{8,16},{12,20},{16,24},{20,28},{1,9},{5,13},{9,17},{1... | collective-permute-start | bytes 1572872 | tf_op jit(solution)/shard_map/ppermute | solution.py:454
  26.4 9.3 %collective-permute-done.1.refs_1_.refs_14_ = f32[256,512]{1,0:T(8,128)S(1)} collective-permute-done((f32[256,512]{1,0:T(8,128)S(1)}, f32[256,512]{1,0:T(8,128)S(1)}, u32[]{:S(2)}, u32[]{:S(2)}) %collective-permute-start.1) | collective-permute-done | bytes 524320 | tf_op jit(solution)/shard_map/ppermute | solution.py:454
  35.8 4.4 %collective-permute-start.2 = (f32[256,512]{1,0:T(8,128)S(1)}, f32[256,512]{1,0:T(8,128)S(1)}, u32[]{:S(2)}, u32[]{:S(2)}) collective-permute-start(f32[256,512]{1,0:T(8,128)S(1)} %collective-permute-done.1.refs_1_.refs_14_), channel_id=1, source_target_pairs={{0,8},{4,12},{8,16},{12,20},{16,24},{20,28},{1,9},{5,13},{9,17},{1... | collective-permute-start | bytes 1572872 | tf_op jit(solution)/shard_map/ppermute | solution.py:454
  41.5 8.3 %collective-permute-done.2.refs_1_.refs_16_ = f32[256,512]{1,0:T(8,128)S(1)} collective-permute-done((f32[256,512]{1,0:T(8,128)S(1)}, f32[256,512]{1,0:T(8,128)S(1)}, u32[]{:S(2)}, u32[]{:S(2)}) %collective-permute-start.2) | collective-permute-done | bytes 524320 | tf_op jit(solution)/shard_map/ppermute | solution.py:454
  50.5 3.8 %collective-permute-done.4.refs_2_.refs_17_ = f32[256,512]{1,0:T(8,128)S(1)} collective-permute-done((f32[256,512]{1,0:T(8,128)S(1)}, f32[256,512]{1,0:T(8,128)S(1)}, u32[]{:S(2)}, u32[]{:S(2)}) %collective-permute-start.4) | collective-permute-done | bytes 524320 | tf_op jit(solution)/shard_map/ppermute | solution.py:454
  54.3 2.6 %collective-permute-start.5 = (f32[128,512]{1,0:T(8,128)S(1)}, f32[128,512]{1,0:T(8,128)S(1)}, u32[]{:S(2)}, u32[]{:S(2)}) collective-permute-start(f32[128,512]{1,0:T(8,128)S(1)} %slice.105), channel_id=1, source_target_pairs={{0,8},{4,12},{8,16},{12,20},{16,24},{20,28},{1,9},{5,13},{9,17},{1... | collective-permute-start | bytes 786440 | tf_op jit(solution)/shard_map/ppermute | solution.py:454
  57.8 2.9 %collective-permute-done.5 = f32[128,512]{1,0:T(8,128)S(1)} collective-permute-done((f32[128,512]{1,0:T(8,128)S(1)}, f32[128,512]{1,0:T(8,128)S(1)}, u32[]{:S(2)}, u32[]{:S(2)}) %collective-permute-start.5) | collective-permute-done | bytes 262176 | tf_op jit(solution)/shard_map/ppermute | solution.py:454
  60.8 5.7 %shard_map.69 = (f32[4,144,128]{2,1,0:T(8,128)S(1)}, f32[4,144,128]{2,1,0:T(8,128)S(1)}) custom-call(s32[9]{0:T(128)S(1)} %concatenate.7.flags, f32[256,2048]{1,0:T(8,128)S(1)} %copy-done.1, f32[256,512]{1,0:T(8,128)S(1)} %pack.1.refs_1_, f32[2,128,128]{2,1,0:T(8,128)S(1)} %get-tuple-element.52.refs_2_, f32[2,8,128]{2,1,0:T(8,128)S(1)} %get-tuple-element.53.refs_3_, ...), custom_call_target="tpu_custom_call" | custom-call | flops 2684354560 | bytes 4194304 | tf_op jit(solution)/shard_map/pallas_call | solution.py:258
  67.0 5.7 %shard_map.71 = (f32[4,144,128]{2,1,0:T(8,128)S(1)}, f32[4,144,128]{2,1,0:T(8,128)S(1)}) custom-call(s32[9]{0:T(128)S(1)} %concatenate.7.flags, f32[256,2048]{1,0:T(8,128)S(1)} %copy-done.1, f32[256,512]{1,0:T(8,128)S(1)} %pack.1.refs_1_, f32[2,128,128]{2,1,0:T(8,128)S(1)} %get-tuple-element.52.refs_2_, f32[2,8,128]{2,1,0:T(8,128)S(1)} %get-tuple-element.53.refs_3_, ...), custom_call_target="tpu_custom_call" | custom-call | flops 2684354560 | bytes 4194304 | tf_op jit(solution)/shard_map/pallas_call | solution.py:258
  72.7 1.7 %collective-permute-start.15 = (f32[4,144,128]{2,1,0:T(8,128)S(1)}, f32[4,144,128]{2,1,0:T(8,128)S(1)}, u32[]{:S(2)}, u32[]{:S(2)}) collective-permute-start(f32[4,144,128]{2,1,0:T(8,128)S(1)} %get-tuple-element.69), channel_id=1, source_target_pairs={{0,4},{4,0},{8,12},{12,8},{16,20},{20,16},{24,28},{28,24},{1,5},{5... | collective-permute-start | bytes 884744 | tf_op jit(solution)/shard_map/ppermute | solution.py:454
  74.4 1.6 %collective-permute-done.8 = f32[4,144,128]{2,1,0:T(8,128)S(1)} collective-permute-done((f32[4,144,128]{2,1,0:T(8,128)S(1)}, f32[4,144,128]{2,1,0:T(8,128)S(1)}, u32[]{:S(2)}, u32[]{:S(2)}) %collective-permute-start.8) | collective-permute-done | bytes 294944 | tf_op jit(solution)/shard_map/ppermute | solution.py:454
  76.0 2.5 %collective-permute-start.9 = (f32[144,128]{1,0:T(8,128)S(1)}, f32[144,128]{1,0:T(8,128)S(1)}, u32[]{:S(2)}, u32[]{:S(2)}) collective-permute-start(f32[144,128]{1,0:T(8,128)S(1)} %get-tuple-element.74), channel_id=1, source_target_pairs={{0,8},{4,12},{8,16},{12,20},{16,24},{20,28},{24,0},{28,4},{1,9},{5... | collective-permute-start | bytes 221192 | tf_op jit(solution)/shard_map/ppermute | solution.py:454
  78.6 2.5 %collective-permute-start.10 = (f32[144,128]{1,0:T(8,128)S(1)}, f32[144,128]{1,0:T(8,128)S(1)}, u32[]{:S(2)}, u32[]{:S(2)}) collective-permute-start(f32[144,128]{1,0:T(8,128)S(1)} %get-tuple-element.73), channel_id=1, source_target_pairs={{0,16},{4,20},{8,24},{12,28},{16,0},{20,4},{24,8},{28,12},{1,17},{... | collective-permute-start | bytes 221192 | tf_op jit(solution)/shard_map/ppermute | solution.py:454
  81.1 2.1 %collective-permute-start.16 = (f32[144,128]{1,0:T(8,128)S(1)}, f32[144,128]{1,0:T(8,128)S(1)}, u32[]{:S(2)}, u32[]{:S(2)}) collective-permute-start(f32[144,128]{1,0:T(8,128)S(1)} %get-tuple-element.78), channel_id=1, source_target_pairs={{0,8},{4,12},{8,16},{12,20},{16,24},{20,28},{24,0},{28,4},{1,9},{5... | collective-permute-start | bytes 221192 | tf_op jit(solution)/shard_map/ppermute | solution.py:454
  83.2 2.4 %collective-permute-done.10.refs_2_ = f32[144,128]{1,0:T(8,128)S(1)} collective-permute-done((f32[144,128]{1,0:T(8,128)S(1)}, f32[144,128]{1,0:T(8,128)S(1)}, u32[]{:S(2)}, u32[]{:S(2)}) %collective-permute-start.10) | collective-permute-done | bytes 73760 | tf_op jit(solution)/shard_map/ppermute | solution.py:454
  88.2 1.9 %collective-permute-start.13 = (f32[152,128]{1,0:T(8,128)S(1)}, f32[152,128]{1,0:T(8,128)S(1)}, u32[]{:S(2)}, u32[]{:S(2)}) collective-permute-start(f32[152,128]{1,0:T(8,128)S(1)} %shard_map.70), channel_id=1, source_target_pairs={{0,16},{4,20},{8,24},{12,28},{16,0},{20,4},{24,8},{28,12},{1,17},{... | collective-permute-start | bytes 233480 | tf_op jit(solution)/shard_map/ppermute | solution.py:454
  90.1 1.8 %collective-permute-start.17 = (f32[144,128]{1,0:T(8,128)S(1)}, f32[144,128]{1,0:T(8,128)S(1)}, u32[]{:S(2)}, u32[]{:S(2)}) collective-permute-start(f32[144,128]{1,0:T(8,128)S(1)} %get-tuple-element.77), channel_id=1, source_target_pairs={{0,16},{4,20},{8,24},{12,28},{16,0},{20,4},{24,8},{28,12},{1,17},{... | collective-permute-start | bytes 221192 | tf_op jit(solution)/shard_map/ppermute | solution.py:454
  91.9 2.2 %collective-permute-start.18 = (f32[144,128]{1,0:T(8,128)S(1)}, f32[144,128]{1,0:T(8,128)S(1)}, u32[]{:S(2)}, u32[]{:S(2)}) collective-permute-start(f32[144,128]{1,0:T(8,128)S(1)} %get-tuple-element.76), channel_id=1, source_target_pairs={{0,24},{4,28},{8,0},{12,4},{16,8},{20,12},{24,16},{28,20},{1,25},{... | collective-permute-start | bytes 221192 | tf_op jit(solution)/shard_map/ppermute | solution.py:454
  94.0 3.7 %collective-permute-done.17.refs_2_ = f32[144,128]{1,0:T(8,128)S(1)} collective-permute-done((f32[144,128]{1,0:T(8,128)S(1)}, f32[144,128]{1,0:T(8,128)S(1)}, u32[]{:S(2)}, u32[]{:S(2)}) %collective-permute-start.17) | collective-permute-done | bytes 73760 | tf_op jit(solution)/shard_map/ppermute | solution.py:454
  98.3 2.0 %collective-permute-start.21 = (f32[152,128]{1,0:T(8,128)S(1)}, f32[152,128]{1,0:T(8,128)S(1)}, u32[]{:S(2)}, u32[]{:S(2)}) collective-permute-start(f32[152,128]{1,0:T(8,128)S(1)} %shard_map.72), channel_id=1, source_target_pairs={{0,24},{4,28},{8,0},{12,4},{16,8},{20,12},{24,16},{28,20},{1,25},{... | collective-permute-start | bytes 233480 | tf_op jit(solution)/shard_map/ppermute | solution.py:454
  100.3 1.7 %collective-permute-start.20 = (f32[152,128]{1,0:T(8,128)S(1)}, f32[152,128]{1,0:T(8,128)S(1)}, u32[]{:S(2)}, u32[]{:S(2)}) collective-permute-start(f32[152,128]{1,0:T(8,128)S(1)} %shard_map.72), channel_id=1, source_target_pairs={{0,16},{4,20},{8,24},{12,28},{16,0},{20,4},{24,8},{28,12},{1,17},{... | collective-permute-start | bytes 233480 | tf_op jit(solution)/shard_map/ppermute | solution.py:454
  102.1 4.7 %collective-permute-start.25 = (f32[4,152,128]{2,1,0:T(8,128)S(1)}, f32[4,152,128]{2,1,0:T(8,128)S(1)}, u32[]{:S(2)}, u32[]{:S(2)}) collective-permute-start(f32[4,152,128]{2,1,0:T(8,128)S(1)} %pad_maximum_fusion.refs_1_), channel_id=1, source_target_pairs={{0,4},{4,0},{8,12},{12,8},{16,20},{20,16},{24,28},{28,24},{1,5},{5... | collective-permute-start | bytes 933896 | tf_op jit(solution)/shard_map/ppermute | solution.py:454
  108.2 4.3 %collective-permute-start.26 = (f32[4,152,128]{2,1,0:T(8,128)S(1)}, f32[4,152,128]{2,1,0:T(8,128)S(1)}, u32[]{:S(2)}, u32[]{:S(2)}) collective-permute-start(f32[4,152,128]{2,1,0:T(8,128)S(1)} %pad_maximum_fusion.1.refs_3_), channel_id=1, source_target_pairs={{0,4},{4,0},{8,12},{12,8},{16,20},{20,16},{24,28},{28,24},{1,5},{5... | collective-permute-start | bytes 933896 | tf_op jit(solution)/shard_map/ppermute | solution.py:454
  113.8 1.5 %collective-permute-start.23 = (f32[8,128]{1,0:T(8,128)S(1)}, f32[8,128]{1,0:T(8,128)S(1)}, u32[]{:S(2)}, u32[]{:S(2)}) collective-permute-start(f32[8,128]{1,0:T(8,128)S(1)} %add.120), channel_id=1, source_target_pairs={{0,2},{1,3},{2,0},{3,1},{4,6},{5,7},{6,4},{7,5},{8,10},{9,11},{10,... | collective-permute-start | bytes 12296 | tf_op jit(solution)/shard_map/ppermute | solution.py:454
  115.3 2.1 %collective-permute-done.23 = f32[8,128]{1,0:T(8,128)S(1)} collective-permute-done((f32[8,128]{1,0:T(8,128)S(1)}, f32[8,128]{1,0:T(8,128)S(1)}, u32[]{:S(2)}, u32[]{:S(2)}) %collective-permute-start.23) | collective-permute-done | bytes 4128 | tf_op jit(solution)/shard_map/ppermute | solution.py:454
  118.1 3.0 %collective-permute-done.24 = f32[8,128]{1,0:T(8,128)S(1)} collective-permute-done((f32[8,128]{1,0:T(8,128)S(1)}, f32[8,128]{1,0:T(8,128)S(1)}, u32[]{:S(2)}, u32[]{:S(2)}) %collective-permute-start.24) | collective-permute-done | bytes 4128 | tf_op jit(solution)/shard_map/ppermute | solution.py:454
  121.1 1.7 %finish.1 = (f32[2048,128]{1,0:T(8,128)}, f32[256,128]{1,0:T(8,128)}) custom-call(s32[2]{0:T(128)S(1)} %pad_add_fusion.where, f32[8,128]{1,0:T(8,128)S(1)} %add.122.refs_0_, f32[4,152,128]{2,1,0:T(8,128)S(1)} %pad_maximum_fusion.refs_1_, f32[4,152,128]{2,1,0:T(8,128)S(1)} %collective-permute-done.25.refs_2_, f32[4,152,128]{2,1,0:T(8,128)S(1)} %pad_maximum_fusion.1.refs_3_, ...), custom_call_target="tpu_custom_call" | custom-call | tf_op jit(solution)/shard_map/finish/pallas_call | solution.py:550
  (65 shorter events, 13.5 us)
Async XLA Ops:
  0.6 1.0 copy-start.2
  2.6 19.1 %collective-permute-start = (f32[256,512]{1,0:T(8,128)S(1)}, f32[256,512]{1,0:T(8,128)S(1)}, u32[]{:S(2)}, u32[]{:S(2)}) collective-permute-start(f32[256,512]{1,0:T(8,128)S(1)} %pack.1.refs_1_), channel_id=1, source_target_pairs={{0,8},{4,12},{8,16},{12,20},{16,24},{20,28},{1,9},{5,13},{9,17},{1... | collective-permute-start | bytes 1572872 | tf_op jit(solution)/shard_map/ppermute | solution.py:454
  7.6 18.2 %collective-permute-start.7 = (f32[256,512]{1,0:T(8,128)S(1)}, f32[256,512]{1,0:T(8,128)S(1)}, u32[]{:S(2)}, u32[]{:S(2)}) collective-permute-start(f32[256,512]{1,0:T(8,128)S(1)} %pack.1.refs_1_), channel_id=1, source_target_pairs={{4,0},{0,4},{12,8},{8,12},{20,16},{16,20},{28,24},{24,28},{5,1},{1... | collective-permute-start | bytes 1572872 | tf_op jit(solution)/shard_map/ppermute | solution.py:454
  9.4 1.6 %copy-start = (f32[256,2048]{1,0:T(8,128)S(1)}, f32[256,2048]{1,0:T(8,128)}, u32[]{:S(2)}) copy-start(f32[256,2048]{1,0:T(8,128)} %refs_0_.7) | copy-start | bytes 6291460
  11.0 3.8 %copy-start.1 = (f32[256,2048]{1,0:T(8,128)S(1)}, f32[256,2048]{1,0:T(8,128)}, u32[]{:S(2)}) copy-start(f32[256,2048]{1,0:T(8,128)} %refs_0_.7) | copy-start | bytes 6291460
  11.0 3.8 %copy-start.4 = (f32[16,128,128]{2,1,0:T(8,128)S(1)}, f32[16,128,128]{2,1,0:T(8,128)}, u32[]{:S(2)}) copy-start(f32[16,128,128]{2,1,0:T(8,128)} %refs_2_.3) | copy-start | bytes 3145732
  11.0 3.8 %copy-start.5 = (f32[2,128,128]{2,1,0:T(8,128)S(1)}, f32[2,128,128]{2,1,0:T(8,128)}, u32[]{:S(2)}) copy-start(f32[2,128,128]{2,1,0:T(8,128)} %refs_3_.7) | copy-start | bytes 393220
  21.7 14.1 %collective-permute-start.1 = (f32[256,512]{1,0:T(8,128)S(1)}, f32[256,512]{1,0:T(8,128)S(1)}, u32[]{:S(2)}, u32[]{:S(2)}) collective-permute-start(f32[256,512]{1,0:T(8,128)S(1)} %collective-permute-done.refs_1_.refs_12_), channel_id=1, source_target_pairs={{0,8},{4,12},{8,16},{12,20},{16,24},{20,28},{1,9},{5,13},{9,17},{1... | collective-permute-start | bytes 1572872 | tf_op jit(solution)/shard_map/ppermute | solution.py:454
  25.2 15.6 %collective-permute-start.6 = (f32[256,512]{1,0:T(8,128)S(1)}, f32[256,512]{1,0:T(8,128)S(1)}, u32[]{:S(2)}, u32[]{:S(2)}) collective-permute-start(f32[256,512]{1,0:T(8,128)S(1)} %collective-permute-done.refs_1_.refs_12_), channel_id=1, source_target_pairs={{4,0},{0,4},{12,8},{8,12},{20,16},{16,20},{28,24},{24,28},{5,1},{1... | collective-permute-start | bytes 1572872 | tf_op jit(solution)/shard_map/ppermute | solution.py:454
  35.8 14.1 %collective-permute-start.2 = (f32[256,512]{1,0:T(8,128)S(1)}, f32[256,512]{1,0:T(8,128)S(1)}, u32[]{:S(2)}, u32[]{:S(2)}) collective-permute-start(f32[256,512]{1,0:T(8,128)S(1)} %collective-permute-done.1.refs_1_.refs_14_), channel_id=1, source_target_pairs={{0,8},{4,12},{8,16},{12,20},{16,24},{20,28},{1,9},{5,13},{9,17},{1... | collective-permute-start | bytes 1572872 | tf_op jit(solution)/shard_map/ppermute | solution.py:454
  40.2 14.1 %collective-permute-start.4 = (f32[256,512]{1,0:T(8,128)S(1)}, f32[256,512]{1,0:T(8,128)S(1)}, u32[]{:S(2)}, u32[]{:S(2)}) collective-permute-start(f32[256,512]{1,0:T(8,128)S(1)} %collective-permute-done.1.refs_1_.refs_14_), channel_id=1, source_target_pairs={{4,0},{0,4},{12,8},{8,12},{20,16},{16,20},{28,24},{24,28},{5,1},{1... | collective-permute-start | bytes 1572872 | tf_op jit(solution)/shard_map/ppermute | solution.py:454
  49.9 7.9 %collective-permute-start.3 = (f32[128,512]{1,0:T(8,128)S(1)}, f32[128,512]{1,0:T(8,128)S(1)}, u32[]{:S(2)}, u32[]{:S(2)}) collective-permute-start(f32[128,512]{1,0:T(8,128)S(1)} %slice.104), channel_id=1, source_target_pairs={{4,0},{0,4},{12,8},{8,12},{20,16},{16,20},{28,24},{24,28},{5,1},{1... | collective-permute-start | bytes 786440 | tf_op jit(solution)/shard_map/ppermute | solution.py:454
  54.3 6.4 %collective-permute-start.5 = (f32[128,512]{1,0:T(8,128)S(1)}, f32[128,512]{1,0:T(8,128)S(1)}, u32[]{:S(2)}, u32[]{:S(2)}) collective-permute-start(f32[128,512]{1,0:T(8,128)S(1)} %slice.105), channel_id=1, source_target_pairs={{0,8},{4,12},{8,16},{12,20},{16,24},{20,28},{1,9},{5,13},{9,17},{1... | collective-permute-start | bytes 786440 | tf_op jit(solution)/shard_map/ppermute | solution.py:454
  66.5 9.5 %collective-permute-start.8 = (f32[4,144,128]{2,1,0:T(8,128)S(1)}, f32[4,144,128]{2,1,0:T(8,128)S(1)}, u32[]{:S(2)}, u32[]{:S(2)}) collective-permute-start(f32[4,144,128]{2,1,0:T(8,128)S(1)} %get-tuple-element.67), channel_id=1, source_target_pairs={{0,4},{4,0},{8,12},{12,8},{16,20},{20,16},{24,28},{28,24},{1,5},{5... | collective-permute-start | bytes 884744 | tf_op jit(solution)/shard_map/ppermute | solution.py:454
  72.7 8.4 %collective-permute-start.15 = (f32[4,144,128]{2,1,0:T(8,128)S(1)}, f32[4,144,128]{2,1,0:T(8,128)S(1)}, u32[]{:S(2)}, u32[]{:S(2)}) collective-permute-start(f32[4,144,128]{2,1,0:T(8,128)S(1)} %get-tuple-element.69), channel_id=1, source_target_pairs={{0,4},{4,0},{8,12},{12,8},{16,20},{20,16},{24,28},{28,24},{1,5},{5... | collective-permute-start | bytes 884744 | tf_op jit(solution)/shard_map/ppermute | solution.py:454
  76.0 7.2 %collective-permute-start.9 = (f32[144,128]{1,0:T(8,128)S(1)}, f32[144,128]{1,0:T(8,128)S(1)}, u32[]{:S(2)}, u32[]{:S(2)}) collective-permute-start(f32[144,128]{1,0:T(8,128)S(1)} %get-tuple-element.74), channel_id=1, source_target_pairs={{0,8},{4,12},{8,16},{12,20},{16,24},{20,28},{24,0},{28,4},{1,9},{5... | collective-permute-start | bytes 221192 | tf_op jit(solution)/shard_map/ppermute | solution.py:454
  78.6 7.1 %collective-permute-start.10 = (f32[144,128]{1,0:T(8,128)S(1)}, f32[144,128]{1,0:T(8,128)S(1)}, u32[]{:S(2)}, u32[]{:S(2)}) collective-permute-start(f32[144,128]{1,0:T(8,128)S(1)} %get-tuple-element.73), channel_id=1, source_target_pairs={{0,16},{4,20},{8,24},{12,28},{16,0},{20,4},{24,8},{28,12},{1,17},{... | collective-permute-start | bytes 221192 | tf_op jit(solution)/shard_map/ppermute | solution.py:454
  81.1 5.8 %collective-permute-start.11 = (f32[144,128]{1,0:T(8,128)S(1)}, f32[144,128]{1,0:T(8,128)S(1)}, u32[]{:S(2)}, u32[]{:S(2)}) collective-permute-start(f32[144,128]{1,0:T(8,128)S(1)} %get-tuple-element.72), channel_id=1, source_target_pairs={{0,24},{4,28},{8,0},{12,4},{16,8},{20,12},{24,16},{28,20},{1,25},{... | collective-permute-start | bytes 221192 | tf_op jit(solution)/shard_map/ppermute | solution.py:454
  81.1 10.8 %collective-permute-start.16 = (f32[144,128]{1,0:T(8,128)S(1)}, f32[144,128]{1,0:T(8,128)S(1)}, u32[]{:S(2)}, u32[]{:S(2)}) collective-permute-start(f32[144,128]{1,0:T(8,128)S(1)} %get-tuple-element.78), channel_id=1, source_target_pairs={{0,8},{4,12},{8,16},{12,20},{16,24},{20,28},{24,0},{28,4},{1,9},{5... | collective-permute-start | bytes 221192 | tf_op jit(solution)/shard_map/ppermute | solution.py:454
  86.9 15.2 %collective-permute-start.14 = (f32[152,128]{1,0:T(8,128)S(1)}, f32[152,128]{1,0:T(8,128)S(1)}, u32[]{:S(2)}, u32[]{:S(2)}) collective-permute-start(f32[152,128]{1,0:T(8,128)S(1)} %shard_map.70), channel_id=1, source_target_pairs={{0,24},{4,28},{8,0},{12,4},{16,8},{20,12},{24,16},{28,20},{1,25},{... | collective-permute-start | bytes 233480 | tf_op jit(solution)/shard_map/ppermute | solution.py:454
  88.2 13.8 %collective-permute-start.13 = (f32[152,128]{1,0:T(8,128)S(1)}, f32[152,128]{1,0:T(8,128)S(1)}, u32[]{:S(2)}, u32[]{:S(2)}) collective-permute-start(f32[152,128]{1,0:T(8,128)S(1)} %shard_map.70), channel_id=1, source_target_pairs={{0,16},{4,20},{8,24},{12,28},{16,0},{20,4},{24,8},{28,12},{1,17},{... | collective-permute-start | bytes 233480 | tf_op jit(solution)/shard_map/ppermute | solution.py:454
  90.1 11.9 %collective-permute-start.12 = (f32[152,128]{1,0:T(8,128)S(1)}, f32[152,128]{1,0:T(8,128)S(1)}, u32[]{:S(2)}, u32[]{:S(2)}) collective-permute-start(f32[152,128]{1,0:T(8,128)S(1)} %shard_map.70), channel_id=1, source_target_pairs={{0,8},{4,12},{8,16},{12,20},{16,24},{20,28},{24,0},{28,4},{1,9},{5... | collective-permute-start | bytes 233480 | tf_op jit(solution)/shard_map/ppermute | solution.py:454
  90.1 7.6 %collective-permute-start.17 = (f32[144,128]{1,0:T(8,128)S(1)}, f32[144,128]{1,0:T(8,128)S(1)}, u32[]{:S(2)}, u32[]{:S(2)}) collective-permute-start(f32[144,128]{1,0:T(8,128)S(1)} %get-tuple-element.77), channel_id=1, source_target_pairs={{0,16},{4,20},{8,24},{12,28},{16,0},{20,4},{24,8},{28,12},{1,17},{... | collective-permute-start | bytes 221192 | tf_op jit(solution)/shard_map/ppermute | solution.py:454
  91.9 6.4 %collective-permute-start.18 = (f32[144,128]{1,0:T(8,128)S(1)}, f32[144,128]{1,0:T(8,128)S(1)}, u32[]{:S(2)}, u32[]{:S(2)}) collective-permute-start(f32[144,128]{1,0:T(8,128)S(1)} %get-tuple-element.76), channel_id=1, source_target_pairs={{0,24},{4,28},{8,0},{12,4},{16,8},{20,12},{24,16},{28,20},{1,25},{... | collective-permute-start | bytes 221192 | tf_op jit(solution)/shard_map/ppermute | solution.py:454
  98.3 8.5 %collective-permute-start.21 = (f32[152,128]{1,0:T(8,128)S(1)}, f32[152,128]{1,0:T(8,128)S(1)}, u32[]{:S(2)}, u32[]{:S(2)}) collective-permute-start(f32[152,128]{1,0:T(8,128)S(1)} %shard_map.72), channel_id=1, source_target_pairs={{0,24},{4,28},{8,0},{12,4},{16,8},{20,12},{24,16},{28,20},{1,25},{... | collective-permute-start | bytes 233480 | tf_op jit(solution)/shard_map/ppermute | solution.py:454
  100.3 6.5 %collective-permute-start.20 = (f32[152,128]{1,0:T(8,128)S(1)}, f32[152,128]{1,0:T(8,128)S(1)}, u32[]{:S(2)}, u32[]{:S(2)}) collective-permute-start(f32[152,128]{1,0:T(8,128)S(1)} %shard_map.72), channel_id=1, source_target_pairs={{0,16},{4,20},{8,24},{12,28},{16,0},{20,4},{24,8},{28,12},{1,17},{... | collective-permute-start | bytes 233480 | tf_op jit(solution)/shard_map/ppermute | solution.py:454
  102.0 6.2 %collective-permute-start.19 = (f32[152,128]{1,0:T(8,128)S(1)}, f32[152,128]{1,0:T(8,128)S(1)}, u32[]{:S(2)}, u32[]{:S(2)}) collective-permute-start(f32[152,128]{1,0:T(8,128)S(1)} %shard_map.72), channel_id=1, source_target_pairs={{0,8},{4,12},{8,16},{12,20},{16,24},{20,28},{24,0},{28,4},{1,9},{5... | collective-permute-start | bytes 233480 | tf_op jit(solution)/shard_map/ppermute | solution.py:454
  102.1 19.0 %collective-permute-start.25 = (f32[4,152,128]{2,1,0:T(8,128)S(1)}, f32[4,152,128]{2,1,0:T(8,128)S(1)}, u32[]{:S(2)}, u32[]{:S(2)}) collective-permute-start(f32[4,152,128]{2,1,0:T(8,128)S(1)} %pad_maximum_fusion.refs_1_), channel_id=1, source_target_pairs={{0,4},{4,0},{8,12},{12,8},{16,20},{20,16},{24,28},{28,24},{1,5},{5... | collective-permute-start | bytes 933896 | tf_op jit(solution)/shard_map/ppermute | solution.py:454
  108.2 12.8 %collective-permute-start.26 = (f32[4,152,128]{2,1,0:T(8,128)S(1)}, f32[4,152,128]{2,1,0:T(8,128)S(1)}, u32[]{:S(2)}, u32[]{:S(2)}) collective-permute-start(f32[4,152,128]{2,1,0:T(8,128)S(1)} %pad_maximum_fusion.1.refs_3_), channel_id=1, source_target_pairs={{0,4},{4,0},{8,12},{12,8},{16,20},{20,16},{24,28},{28,24},{1,5},{5... | collective-permute-start | bytes 933896 | tf_op jit(solution)/shard_map/ppermute | solution.py:454
  112.6 1.2 collective-permute-start.22
  113.8 3.6 %collective-permute-start.23 = (f32[8,128]{1,0:T(8,128)S(1)}, f32[8,128]{1,0:T(8,128)S(1)}, u32[]{:S(2)}, u32[]{:S(2)}) collective-permute-start(f32[8,128]{1,0:T(8,128)S(1)} %add.120), channel_id=1, source_target_pairs={{0,2},{1,3},{2,0},{3,1},{4,6},{5,7},{6,4},{7,5},{8,10},{9,11},{10,... | collective-permute-start | bytes 12296 | tf_op jit(solution)/shard_map/ppermute | solution.py:454
  117.4 3.6 %collective-permute-start.24 = (f32[8,128]{1,0:T(8,128)S(1)}, f32[8,128]{1,0:T(8,128)S(1)}, u32[]{:S(2)}, u32[]{:S(2)}) collective-permute-start(f32[8,128]{1,0:T(8,128)S(1)} %add.121), channel_id=1, source_target_pairs={{0,4},{4,0},{8,12},{12,8},{16,20},{20,16},{24,28},{28,24},{1,5},{5... | collective-permute-start | bytes 12296 | tf_op jit(solution)/shard_map/ppermute | solution.py:454
  (1 other events, 0.9 us)
